TPU v7x, 32 devices: a whole 2x2x4 slice. The times are simulated.
32 devices in a mesh: tm: 2 (over y), space: 16 (over z, x, core).
Axes of the slice: x: 2, y: 2, z: 4, core: 2. Of those that a mesh axis runs over, the one named last changes fastest.
Arguments:
- control: float32 [32, 51200], P(('tm', 'space')), may hold values from -4 to 4
- spectrum: float32 [51200], replicated, may hold values from 0.2 to 2
- perturb: bfloat16 [4, 32, 4, 51200], P('tm', None, None, 'space'), may hold values from -1 to 1
- obs_index: int32 [4, 32768], P('tm', 'space'), may hold values from 0 to 12799
- innovation: float32 [4, 32768], P('tm', 'space'), may hold values from -10 to 10
- obs_sigma: float32 [4, 32768], P('tm', 'space'), may hold values from 0.5 to 2
- qc_class: int32 [4, 32768], P('tm', 'space'), may hold values from 0 to 2
Outputs:
- control_out: float32 [32, 51200], P(('tm', 'space'))
- cost_list: float32 [1], replicated
Inputs may be any that keep to these rules, and one draw needn't show every extreme that they name: `obs_index`: observation o of block o // 2048 observes the cell level * 3200 + point, the point counted within the block's piece of the grid; repeats may occur.
All inputs are finite; a program needn't handle non-finite values.
Results may differ from a plain program's by a relative error of at most 0.0034.
Values may be sent and summed in bfloat16 or wider, within the bound.
A program may use at most 128 MiB of HBM per device.

v0:
```python
import jax
import jax.numpy as jnp
from jax import lax
from jax.sharding import PartitionSpec as P

GX = 320
GY = 160


def lookup_tables(segment_length):
    wave_num = jnp.arange(segment_length, dtype=jnp.float32)[:, None]
    grid_positions = jnp.arange(segment_length, dtype=jnp.float32)[None, :]
    basis = jnp.cos(jnp.pi * (grid_positions + 0.5) * wave_num / segment_length) * jnp.sqrt(
        2.0 / segment_length
    )
    return jnp.where(wave_num == 0, basis * jnp.sqrt(0.5), basis)


def synthesize(control, spectrum, basis_x, basis_y):
    coeffs = (control * spectrum[None, :]).reshape(control.shape[0], GX, GY)
    middle = jnp.einsum("kn,mkl->mnl", basis_x, coeffs, precision=lax.Precision.HIGHEST)
    result = jnp.einsum("mnl,lp->mnp", middle, basis_y, precision=lax.Precision.HIGHEST)
    return result.reshape(control.shape[0], GX * GY)


def analyze(adjoint, spectrum, basis_x, basis_y):
    state_fields = adjoint.reshape(adjoint.shape[0], GX, GY)
    middle = jnp.einsum("kn,mnp->mkp", basis_x, state_fields, precision=lax.Precision.HIGHEST)
    result = jnp.einsum("mkp,lp->mkl", middle, basis_y, precision=lax.Precision.HIGHEST)
    return result.reshape(adjoint.shape[0], GX * GY) * spectrum[None, :]


def per_device(control, spectrum, perturb, obs_index, innovation, obs_sigma, qc_class):
    basis_x = lookup_tables(GX)
    basis_y = lookup_tables(GY)
    slot_count = perturb.shape[0]
    levels = perturb.shape[2]
    piece_len = perturb.shape[3]
    radius = jnp.where(qc_class == 0, 4.0, jnp.where(qc_class == 1, 2.0, 1.0)).astype(jnp.float32)

    def scatter_cells(indices, values):
        return jnp.zeros((levels * piece_len,), jnp.float32).at[indices].add(values)

    member_field = synthesize(control, spectrum, basis_x, basis_y).astype(jnp.bfloat16)
    pieces = lax.all_to_all(member_field, "space", split_axis=1, concat_axis=0, tiled=True)
    selected_entries = perturb
    increment = jnp.einsum(
        "dzab,zb->dab",
        selected_entries,
        lax.all_gather(pieces, "tm", axis=0, tiled=True),
        preferred_element_type=jnp.float32,
    )
    cells_flat = increment.reshape(slot_count, levels * piece_len)
    modelled = jnp.take_along_axis(cells_flat, obs_index, axis=1)
    scaled = (modelled - innovation) / obs_sigma
    scaled_sq = scaled * scaled / (radius * radius)
    obs_part = jnp.sum(0.5 * radius * radius * jnp.log1p(scaled_sq))
    back_part = 0.5 * jnp.sum(control * control)
    obs_grad = scaled / ((1.0 + scaled_sq) * obs_sigma)
    control_update = jax.vmap(scatter_cells)(obs_index, obs_grad).astype(jnp.bfloat16)
    control_update = control_update.reshape(slot_count, levels, piece_len)
    selected_entries = perturb
    summed_rows = lax.psum_scatter(
        jnp.einsum(
            "qiyr,qyr->ir", selected_entries, control_update, preferred_element_type=jnp.float32
        ).astype(jnp.bfloat16),
        "tm",
        scatter_dimension=0,
        tiled=True,
    ).astype(jnp.float32)
    adjoint = lax.all_to_all(
        summed_rows.astype(jnp.bfloat16), "space", split_axis=0, concat_axis=1, tiled=True
    ).astype(summed_rows.dtype)
    gradient = control + analyze(adjoint, spectrum, basis_x, basis_y)
    grad_part = jnp.sum(gradient * gradient)
    obs_cost, back_cost = lax.psum((obs_part, back_part), ("tm", "space"))
    grad_sq = lax.psum(grad_part, ("tm", "space"))
    total_cost = back_cost + obs_cost
    step_size = 0.5 * total_cost / (grad_sq + 1e-06)
    control = control - step_size * gradient
    cost_list = [total_cost]
    return (control, jnp.stack(cost_list))


def solution(mesh):
    in_specs = (
        P(("tm", "space"), None),
        P(),
        P("tm", None, None, "space"),
        P("tm", "space"),
        P("tm", "space"),
        P("tm", "space"),
        P("tm", "space"),
    )
    out_specs = (P(("tm", "space"), None), P())
    return jax.shard_map(
        per_device, mesh=mesh, in_specs=in_specs, out_specs=out_specs, check_vma=False
    )
```

profile of v0, /device:TPU:12, one launch (start us, length us, event | category | flops | bytes accessed | tf_op | source)
XLA Modules:
  0.0 175.2 jit_solution(5619311376740743592)
XLA Ops:
  7.2 2.4 %multiply_reduce_fusion.4 = (f32[]{:T(128)}, f32[51200]{0:T(1024)S(1)}) fusion(f32[1,51200]{1,0:T(1,128)} %param.7, f32[1,51200]{1,0:T(1,128)} %bitcast.56), kind=kLoop, calls=%fused_computation.23 | loop fusion | flops 153599 | bytes 614404 | tf_op jit(solution)/shard_map/reduce_sum | solution.py:58
  9.6 0.0 copy-start.3
  9.6 0.0 copy-start.7
  9.6 0.0 copy-start.8
  9.6 0.1 reshape.98
  9.8 2.6 %convolution_bitcast_fusion.1 = f32[320,160]{0,1:T(8,128)S(1)} fusion(f32[320,160]{1,0:T(8,128)S(1)} %reshape.98, f32[320]{0:T(512)S(1)} %add_multiply_fusion, pred[320]{0:T(512)(128)(4,1)S(1)} %iota_compare_fusion), kind=kOutput, calls=%fused_computation.5 | convolution fusion | flops 197120000 | bytes 411200 | tf_op jit(solution)/shard_map/kn,mkl->mnl/dot_general | solution.py:21
  12.4 1.1 convolution_convert_fusion
  13.4 0.0 copy-start
  13.5 0.1 copy.14
  13.6 0.3 convert_element_type.33
  13.9 0.5 broadcast.94
  14.4 1.2 reduce.13
  15.5 0.8 reshape.139
  16.3 6.3 %all-to-all-start = ((bf16[16,2,1600]{2,1,0:T(2,128)(2,1)}), bf16[16,2,1600]{2,1,0:T(2,128)(2,1)S(1)}, u32[]{:S(2)}, u32[]{:S(2)}) async-start(bf16[16,2,1600]{2,1,0:T(2,128)(2,1)} %reshape.139), calls=%async_computation | async-start | bytes 212992 | tf_op jit(solution)/shard_map/all_to_all | solution.py:45
  22.6 0.0 reduce-scatter.2.cloned.1.call-start
  22.7 0.0 copy-done.3
  22.7 0.0 copy-done.7
  22.7 0.1 multiply_reduce_fusion.5
  22.8 0.0 copy-done.8
  22.8 0.1 and_reduce_fusion
  23.0 4.9 %all-to-all-done = bf16[16,2,1600]{2,1,0:T(2,128)(2,1)S(1)} async-done(((bf16[16,2,1600]{2,1,0:T(2,128)(2,1)}), bf16[16,2,1600]{2,1,0:T(2,128)(2,1)S(1)}, u32[]{:S(2)}, u32[]{:S(2)}) %all-to-all-start) | async-done | bytes 102432 | tf_op jit(solution)/shard_map/all_to_all | solution.py:45
  27.9 0.2 reshape.140
  28.1 5.8 %all-gather = bf16[1,32,3200]{2,1,0:T(8,128)(2,1)S(1)} all-gather(bf16[1,16,3200]{2,1,0:T(8,128)(2,1)S(1)} %copy.16), channel_id=2, replica_groups=mesh['tm'=2,'space'=16] {'tm'}, dimensions={1}, use_global_device_ids=true | all-gather | bytes 307200 | tf_op jit(solution)/shard_map/all_gather | solution.py:50
  34.0 0.0 copy-done
  34.0 0.9 multiply_reduce_fusion.1
  34.8 0.1 copy.36
  34.9 0.0 copy-start.4
  34.9 0.0 copy-start.5
  34.9 0.0 copy-start.6
  34.9 34.9 %gather_fusion = f32[4096]{0:T(1024)S(1)} fusion(f32[2,12800]{1,0:T(2,128)S(1)} %bitcast.52, s32[4096]{0:T(1024)S(1)} %bitcast.53), kind=kCustom, calls=%fused_computation | custom fusion | bytes 65536 | tf_op jit(solution)/shard_map/jit(take_along_axis)/gather | solution.py:54
  69.9 0.0 copy-done.4
  69.9 0.0 copy-done.5
  69.9 0.0 copy-done.6
  69.9 0.8 fusion.26
  70.7 21.9 %scatter_custom_fusion = f32[25600]{0:T(1024)S(1)} fusion(s32[4096]{0:T(1024)S(1)} %bitcast.61, f32[4096]{0:T(1024)S(1)} %bitcast.62, f32[]{:T(128)} %constant.17.clone.1), kind=kCustom, calls=%fused_computation.39 | custom fusion | flops 4096 | bytes 102404
  92.7 2.2 %multiply_reduce_fusion = bf16[3200,32]{0,1:T(8,128)(2,1)} fusion(f32[3200,2,4]{0,2,1:T(4,128)S(1)} %bitcast_convert_fusion.1, bf16[2,32,4,3200]{3,2,1,0:T(4,128)(2,1)S(1)} %copy-done), kind=kLoop, calls=%fused_computation.2 | loop fusion | flops 2355200 | bytes 1945600 | tf_op jit(solution)/shard_map/qiyr,qyr->ir/dot_general | solution.py:64
  94.9 0.0 reduce-scatter.2.cloned.1.call-update
  94.9 9.4 %reduce-scatter.2.cloned.1.call-done = bf16[16,3200]{1,0:T(8,128)(2,1)} async-done(((bf16[32,3200]{1,0:T(8,128)(2,1)}), bf16[16,3200]{1,0:T(8,128)(2,1)}) %reduce-scatter.2.cloned.1.call-update) | async-done | bytes 102416 | tf_op jit(solution)/shard_map/reduce_scatter | solution.py:63
  104.3 1.5 reduce.14
  105.8 0.8 reshape.141
  106.6 0.0 copy-start.2
  106.6 6.2 %all-to-all-start.1 = ((bf16[16,2,1600]{2,1,0:T(2,128)(2,1)}), bf16[16,2,1600]{2,1,0:T(2,128)(2,1)S(1)}, u32[]{:S(2)}, u32[]{:S(2)}) async-start(bf16[16,2,1600]{2,1,0:T(2,128)(2,1)} %reshape.141), calls=%async_computation.2 | async-start | bytes 212992 | tf_op jit(solution)/shard_map/all_to_all | solution.py:71
  114.2 3.9 %all-to-all-done.1 = bf16[16,2,1600]{2,1,0:T(2,128)(2,1)S(1)} async-done(((bf16[16,2,1600]{2,1,0:T(2,128)(2,1)}), bf16[16,2,1600]{2,1,0:T(2,128)(2,1)S(1)}, u32[]{:S(2)}, u32[]{:S(2)}) %all-to-all-start.1) | async-done | bytes 102432 | tf_op jit(solution)/shard_map/all_to_all | solution.py:71
  118.1 0.2 reshape.142
  118.3 0.0 copy-start.1
  118.3 0.6 reduce.5
  118.9 0.2 reshape.103
  119.1 2.3 %convolution_bitcast_fusion = f32[320,160]{0,1:T(8,128)S(1)} fusion(bf16[320,160]{1,0:T(8,128)(2,1)S(1)} %reshape.103, f32[320]{0:T(512)S(1)} %add_multiply_fusion, pred[320]{0:T(512)(128)(4,1)S(1)} %iota_compare_fusion), kind=kOutput, calls=%fused_computation.4 | convolution fusion | flops 197120000 | bytes 308800 | tf_op jit(solution)/shard_map/kn,mnp->mkp/dot_general | solution.py:28
  121.4 1.3 fusion.10
  122.7 0.3 reshape.105
  123.0 0.0 copy-done.2
  123.0 0.0 copy-done.1
  123.0 1.0 multiply_reduce_fusion.2
  124.1 42.1 %all-reduce = (f32[]{:T(128)}, f32[]{:T(128)}) all-reduce(f32[]{:T(128)S(6)} %add.65, f32[]{:T(128)} %get-tuple-element.6), channel_id=1, replica_groups=mesh['tm'=2,'space'=16] {'tm','space'}, use_global_device_ids=true, to_apply=%region_1.2 | all-reduce | flops 2 | bytes 16 | tf_op jit(solution)/shard_map/psum | solution.py:76
  167.5 0.9 multiply_subtract_fusion
  (19 shorter events, 0.3 us)
Async XLA Ops:
  9.6 13.0 %copy-start.3 = (s32[2,2048]{1,0:T(2,128)S(1)}, s32[2,2048]{1,0:T(2,128)}, u32[]{:S(2)}) copy-start(s32[2,2048]{1,0:T(2,128)} %param.10) | copy-start | bytes 49156
  9.6 13.1 %copy-start.7 = (s32[2]{0:T(128)S(1)}, s32[2]{0:T(128)}, u32[]{:S(2)}) copy-start(s32[2]{0:T(128)} %constant.15) | copy-start | bytes 28
  9.6 13.2 %copy-start.8 = (s32[2]{0:T(128)S(1)}, s32[2]{0:T(128)}, u32[]{:S(2)}) copy-start(s32[2]{0:T(128)} %constant.61) | copy-start | bytes 28
  13.4 20.5 %copy-start = (bf16[2,32,4,3200]{3,2,1,0:T(4,128)(2,1)S(1)}, bf16[2,32,4,3200]{3,2,1,0:T(4,128)(2,1)}, u32[]{:S(2)}) copy-start(bf16[2,32,4,3200]{3,2,1,0:T(4,128)(2,1)} %param.9) | copy-start | bytes 4915204
  16.3 11.6 %all-to-all-start = ((bf16[16,2,1600]{2,1,0:T(2,128)(2,1)}), bf16[16,2,1600]{2,1,0:T(2,128)(2,1)S(1)}, u32[]{:S(2)}, u32[]{:S(2)}) async-start(bf16[16,2,1600]{2,1,0:T(2,128)(2,1)} %reshape.139), calls=%async_computation | async-start | bytes 212992 | tf_op jit(solution)/shard_map/all_to_all | solution.py:45
  22.6 81.7 %reduce-scatter.2.cloned.1.call-start = ((), (), s32[]{:S(2)}) async-start(), calls=%async_computation.3 | async-start | bytes 307200 | tf_op jit(solution)/shard_map/reduce_scatter | solution.py:63
  34.9 35.0 %copy-start.4 = (f32[2,2048]{1,0:T(2,128)S(1)}, f32[2,2048]{1,0:T(2,128)}, u32[]{:S(2)}) copy-start(f32[2,2048]{1,0:T(2,128)} %param.12) | copy-start | bytes 49156
  34.9 35.0 %copy-start.5 = (f32[2,2048]{1,0:T(2,128)S(1)}, f32[2,2048]{1,0:T(2,128)}, u32[]{:S(2)}) copy-start(f32[2,2048]{1,0:T(2,128)} %param.11) | copy-start | bytes 49156
  34.9 35.0 %copy-start.6 = (s32[2,2048]{1,0:T(2,128)S(1)}, s32[2,2048]{1,0:T(2,128)}, u32[]{:S(2)}) copy-start(s32[2,2048]{1,0:T(2,128)} %param.13) | copy-start | bytes 49156
  106.6 16.4 %copy-start.2 = (f32[51200]{0:T(1024)S(1)}, f32[51200]{0:T(1024)}, u32[]{:S(2)}) copy-start(f32[51200]{0:T(1024)} %param.8) | copy-start | bytes 614404
  106.6 11.5 %all-to-all-start.1 = ((bf16[16,2,1600]{2,1,0:T(2,128)(2,1)}), bf16[16,2,1600]{2,1,0:T(2,128)(2,1)S(1)}, u32[]{:S(2)}, u32[]{:S(2)}) async-start(bf16[16,2,1600]{2,1,0:T(2,128)(2,1)} %reshape.141), calls=%async_computation.2 | async-start | bytes 212992 | tf_op jit(solution)/shard_map/all_to_all | solution.py:71
  118.3 4.8 %copy-start.1 = (f32[1,51200]{1,0:T(1,128)S(1)}, f32[1,51200]{1,0:T(1,128)}, u32[]{:S(2)}) copy-start(f32[1,51200]{1,0:T(1,128)} %param.7) | copy-start | bytes 614404
Sparse Core Ops, SparseCore 0:
  95.0 9.2 reduce-scatter.1
where the time goes:
time: 176 us; the launch traced here: 175 us
  blocking collectives  47.9 us (27%)
  local copies, waits for them, and re-layouts  38.5 us (22%)
  other arithmetic  33.7 us (19%)
  waiting for transfers between devices  18.3 us (10%)
  between operations  17 us (10%)
  starting transfers between devices  12.5 us (7%)
  matrix products  7.25 us (4%)
    psum x1, blocking collectives, per_device(): obs_cost, back_cost = lax.psum((obs_part, back_part), ('tm', 'space'))  42.1 us
    gather x3, local copies, waits for them, and re-layouts, per_device(): modelled = jnp.take_along_axis(cells_flat, obs_index, axis=1)  34.9 us
    unnamed x9, other arithmetic  23.4 us
    reduce_scatter x1, waiting for transfers between devices, per_device(): lax.psum_scatter(jnp.einsum('qiyr,qyr->ir', selected_entries, control_upd...  9.45 us
    all_to_all x1, starting transfers between devices, per_device(): lax.all_to_all(member_field, 'space', split_axis=1, concat_axis=0, tiled=...  6.27 us
    all_to_all x1, starting transfers between devices, per_device(): lax.all_to_all(summed_rows.astype(jnp.bfloat16), 'space', split_axis=0, c...  6.2 us
    all_gather x1, blocking collectives, per_device(): lax.all_gather(pieces, 'tm', axis=0, tiled=True)  5.84 us
    all_to_all x1, waiting for transfers between devices, per_device(): lax.all_to_all(member_field, 'space', split_axis=1, concat_axis=0, tiled=...  4.91 us
  transfers between devices with their start and end apart: 3, of which 3 were waited for; matrix products, arithmetic and copies ran while one was open for 0% of the time, Pallas kernels for 0%

commit v1 on v0

--- a/solution.py
+++ b/solution.py
@@ -73,7 +73,7 @@
     ).astype(summed_rows.dtype)
     gradient = control + analyze(adjoint, spectrum, basis_x, basis_y)
     grad_part = jnp.sum(gradient * gradient)
-    obs_cost, back_cost = lax.psum((obs_part, back_part), ("tm", "space"))
+    obs_cost, back_cost = lax.psum(lax.psum((obs_part, back_part), "space"), "tm")
     grad_sq = lax.psum(grad_part, ("tm", "space"))
     total_cost = back_cost + obs_cost
     step_size = 0.5 * total_cost / (grad_sq + 1e-06)

time: 176 us -> 210 us (1.19)
  blocking collectives: 47.9 us -> 85.7 us
  waiting for transfers between devices: 18.3 us -> 14.4 us
    psum x1 -> x3, blocking collectives: 42.1 us -> 79.9 us  [the longest x1 48.2 us: per_device(): grad_sq = lax.psum(grad_part, ('tm', 'space'))]
    all_to_all x1, waiting for transfers between devices: 3.95 us -> 0.01 us  [per_device(): lax.all_to_all(summed_rows.astype(jnp.bfloat16), 'space', split_axis=0, c...]
  transfers between devices with their start and end apart: 3 -> 3, of which waited for: 3 -> 2; matrix products, arithmetic and copies ran while one was open for 0% -> 0% of each run, Pallas kernels for 0% -> 0%
where the time goes in v1:
time: 210 us; the launch traced here: 209 us
  blocking collectives  85.7 us (41%)
  local copies, waits for them, and re-layouts  38.5 us (18%)
  other arithmetic  33.7 us (16%)
  between operations  17 us (8%)
  waiting for transfers between devices  14.4 us (7%)
  starting transfers between devices  12.5 us (6%)
  matrix products  7.25 us (3%)
    psum x1, blocking collectives, per_device(): grad_sq = lax.psum(grad_part, ('tm', 'space'))  48.2 us
    gather x3, local copies, waits for them, and re-layouts, per_device(): modelled = jnp.take_along_axis(cells_flat, obs_index, axis=1)  34.9 us
    psum x1, blocking collectives, per_device(): lax.psum((obs_part, back_part), 'space')  26 us
    unnamed x9, other arithmetic  23.4 us
    reduce_scatter x1, waiting for transfers between devices, per_device(): lax.psum_scatter(jnp.einsum('qiyr,qyr->ir', selected_entries, control_upd...  9.45 us
    all_to_all x1, starting transfers between devices, per_device(): lax.all_to_all(member_field, 'space', split_axis=1, concat_axis=0, tiled=...  6.27 us
    all_to_all x1, starting transfers between devices, per_device(): lax.all_to_all(summed_rows.astype(jnp.bfloat16), 'space', split_axis=0, c...  6.2 us
    all_gather x1, blocking collectives, per_device(): lax.all_gather(pieces, 'tm', axis=0, tiled=True)  5.84 us
  transfers between devices with their start and end apart: 3, of which 2 were waited for; matrix products, arithmetic and copies ran while one was open for 0% of the time, Pallas kernels for 0%

profile of v1, /device:TPU:12, one launch (start us, length us, event | category | flops | bytes accessed | tf_op | source)
XLA Modules:
  0.0 209.1 jit_solution(17337884691341287149)
XLA Ops:
  7.2 2.4 %multiply_reduce_fusion.4 = (f32[]{:T(128)}, f32[51200]{0:T(1024)S(1)}) fusion(f32[1,51200]{1,0:T(1,128)} %param.7, f32[1,51200]{1,0:T(1,128)} %bitcast.56), kind=kLoop, calls=%fused_computation.23 | loop fusion | flops 153599 | bytes 614404 | tf_op jit(solution)/shard_map/reduce_sum | solution.py:58
  9.6 0.0 copy-start.3
  9.6 0.0 copy-start.7
  9.6 0.0 copy-start.8
  9.6 0.1 reshape.98
  9.8 2.6 %convolution_bitcast_fusion.1 = f32[320,160]{0,1:T(8,128)S(1)} fusion(f32[320,160]{1,0:T(8,128)S(1)} %reshape.98, f32[320]{0:T(512)S(1)} %add_multiply_fusion, pred[320]{0:T(512)(128)(4,1)S(1)} %iota_compare_fusion), kind=kOutput, calls=%fused_computation.5 | convolution fusion | flops 197120000 | bytes 411200 | tf_op jit(solution)/shard_map/kn,mkl->mnl/dot_general | solution.py:21
  12.4 1.1 convolution_convert_fusion
  13.4 0.0 copy-start
  13.5 0.1 copy.14
  13.6 0.3 convert_element_type.33
  13.9 0.5 broadcast.94
  14.4 1.2 reduce.13
  15.5 0.8 reshape.139
  16.3 6.3 %all-to-all-start = ((bf16[16,2,1600]{2,1,0:T(2,128)(2,1)}), bf16[16,2,1600]{2,1,0:T(2,128)(2,1)S(1)}, u32[]{:S(2)}, u32[]{:S(2)}) async-start(bf16[16,2,1600]{2,1,0:T(2,128)(2,1)} %reshape.139), calls=%async_computation | async-start | bytes 212992 | tf_op jit(solution)/shard_map/all_to_all | solution.py:45
  22.6 0.0 reduce-scatter.2.cloned.1.call-start
  22.7 0.0 copy-done.3
  22.7 0.0 copy-done.7
  22.7 0.1 multiply_reduce_fusion.5
  22.8 0.0 copy-done.8
  22.8 0.1 and_reduce_fusion
  23.0 4.9 %all-to-all-done = bf16[16,2,1600]{2,1,0:T(2,128)(2,1)S(1)} async-done(((bf16[16,2,1600]{2,1,0:T(2,128)(2,1)}), bf16[16,2,1600]{2,1,0:T(2,128)(2,1)S(1)}, u32[]{:S(2)}, u32[]{:S(2)}) %all-to-all-start) | async-done | bytes 102432 | tf_op jit(solution)/shard_map/all_to_all | solution.py:45
  27.9 0.2 reshape.140
  28.1 5.8 %all-gather = bf16[1,32,3200]{2,1,0:T(8,128)(2,1)S(1)} all-gather(bf16[1,16,3200]{2,1,0:T(8,128)(2,1)S(1)} %copy.16), channel_id=2, replica_groups=mesh['tm'=2,'space'=16] {'tm'}, dimensions={1}, use_global_device_ids=true | all-gather | bytes 307200 | tf_op jit(solution)/shard_map/all_gather | solution.py:50
  34.0 0.0 copy-done
  34.0 0.9 multiply_reduce_fusion.1
  34.8 0.1 copy.36
  34.9 0.0 copy-start.4
  34.9 0.0 copy-start.5
  34.9 0.0 copy-start.6
  34.9 34.9 %gather_fusion = f32[4096]{0:T(1024)S(1)} fusion(f32[2,12800]{1,0:T(2,128)S(1)} %bitcast.52, s32[4096]{0:T(1024)S(1)} %bitcast.53), kind=kCustom, calls=%fused_computation | custom fusion | bytes 65536 | tf_op jit(solution)/shard_map/jit(take_along_axis)/gather | solution.py:54
  69.9 0.0 copy-done.4
  69.9 0.0 copy-done.5
  69.9 0.0 copy-done.6
  69.9 0.8 fusion.26
  70.7 21.9 %scatter_custom_fusion = f32[25600]{0:T(1024)S(1)} fusion(s32[4096]{0:T(1024)S(1)} %bitcast.61, f32[4096]{0:T(1024)S(1)} %bitcast.62, f32[]{:T(128)} %constant.17.clone.1), kind=kCustom, calls=%fused_computation.39 | custom fusion | flops 4096 | bytes 102404
  92.7 2.2 %multiply_reduce_fusion = bf16[3200,32]{0,1:T(8,128)(2,1)} fusion(f32[3200,2,4]{0,2,1:T(4,128)S(1)} %bitcast_convert_fusion.1, bf16[2,32,4,3200]{3,2,1,0:T(4,128)(2,1)S(1)} %copy-done), kind=kLoop, calls=%fused_computation.2 | loop fusion | flops 2355200 | bytes 1945600 | tf_op jit(solution)/shard_map/qiyr,qyr->ir/dot_general | solution.py:64
  94.9 0.0 reduce-scatter.2.cloned.1.call-update
  94.9 9.4 %reduce-scatter.2.cloned.1.call-done = bf16[16,3200]{1,0:T(8,128)(2,1)} async-done(((bf16[32,3200]{1,0:T(8,128)(2,1)}), bf16[16,3200]{1,0:T(8,128)(2,1)}) %reduce-scatter.2.cloned.1.call-update) | async-done | bytes 102416 | tf_op jit(solution)/shard_map/reduce_scatter | solution.py:63
  104.3 1.5 reduce.14
  105.8 0.8 reshape.141
  106.6 0.0 copy-start.2
  106.6 6.2 %all-to-all-start.1 = ((bf16[16,2,1600]{2,1,0:T(2,128)(2,1)}), bf16[16,2,1600]{2,1,0:T(2,128)(2,1)S(1)}, u32[]{:S(2)}, u32[]{:S(2)}) async-start(bf16[16,2,1600]{2,1,0:T(2,128)(2,1)} %reshape.141), calls=%async_computation.2 | async-start | bytes 212992 | tf_op jit(solution)/shard_map/all_to_all | solution.py:71
  114.2 26.0 %psum.41 = f32[]{:T(128)} all-reduce(f32[]{:T(128)S(6)} %add.69), channel_id=1, replica_groups=mesh['tm'=2,'space'=16] {'space'}, use_global_device_ids=true, to_apply=%region_1.2 | all-reduce | flops 1 | bytes 8 | tf_op jit(solution)/shard_map/psum | solution.py:76
  140.1 5.7 %psum.40 = f32[]{:T(128)} all-reduce(f32[]{:T(128)} %psum.41), channel_id=1, replica_groups=mesh['tm'=2,'space'=16] {'tm'}, use_global_device_ids=true, to_apply=%region_2.3 | all-reduce | flops 1 | bytes 8 | tf_op jit(solution)/shard_map/psum | solution.py:76
  146.5 0.0 all-to-all-done.1
  146.5 0.2 reshape.142
  146.7 0.0 copy-start.1
  146.7 0.6 reduce.5
  147.3 0.2 reshape.103
  147.5 2.3 %convolution_bitcast_fusion = f32[320,160]{0,1:T(8,128)S(1)} fusion(bf16[320,160]{1,0:T(8,128)(2,1)S(1)} %reshape.103, f32[320]{0:T(512)S(1)} %add_multiply_fusion, pred[320]{0:T(512)(128)(4,1)S(1)} %iota_compare_fusion), kind=kOutput, calls=%fused_computation.4 | convolution fusion | flops 197120000 | bytes 308800 | tf_op jit(solution)/shard_map/kn,mnp->mkp/dot_general | solution.py:28
  149.8 1.3 fusion.10
  151.1 0.3 reshape.105
  151.4 0.0 copy-done.2
  151.5 0.0 copy-done.1
  151.5 1.0 multiply_reduce_fusion.2
  152.5 48.2 %psum.39 = f32[]{:T(128)} all-reduce(f32[]{:T(128)} %get-tuple-element.4), channel_id=1, replica_groups=mesh['tm'=2,'space'=16] {'tm','space'}, use_global_device_ids=true, to_apply=%region_9.10 | all-reduce | flops 1 | bytes 8 | tf_op jit(solution)/shard_map/psum | solution.py:77
  201.4 0.9 multiply_subtract_fusion
  (19 shorter events, 0.3 us)
Async XLA Ops:
  9.6 13.0 %copy-start.3 = (s32[2,2048]{1,0:T(2,128)S(1)}, s32[2,2048]{1,0:T(2,128)}, u32[]{:S(2)}) copy-start(s32[2,2048]{1,0:T(2,128)} %param.10) | copy-start | bytes 49156
  9.6 13.1 %copy-start.7 = (s32[2]{0:T(128)S(1)}, s32[2]{0:T(128)}, u32[]{:S(2)}) copy-start(s32[2]{0:T(128)} %constant.15) | copy-start | bytes 28
  9.6 13.2 %copy-start.8 = (s32[2]{0:T(128)S(1)}, s32[2]{0:T(128)}, u32[]{:S(2)}) copy-start(s32[2]{0:T(128)} %constant.61) | copy-start | bytes 28
  13.4 20.5 %copy-start = (bf16[2,32,4,3200]{3,2,1,0:T(4,128)(2,1)S(1)}, bf16[2,32,4,3200]{3,2,1,0:T(4,128)(2,1)}, u32[]{:S(2)}) copy-start(bf16[2,32,4,3200]{3,2,1,0:T(4,128)(2,1)} %param.9) | copy-start | bytes 4915204
  16.3 11.6 %all-to-all-start = ((bf16[16,2,1600]{2,1,0:T(2,128)(2,1)}), bf16[16,2,1600]{2,1,0:T(2,128)(2,1)S(1)}, u32[]{:S(2)}, u32[]{:S(2)}) async-start(bf16[16,2,1600]{2,1,0:T(2,128)(2,1)} %reshape.139), calls=%async_computation | async-start | bytes 212992 | tf_op jit(solution)/shard_map/all_to_all | solution.py:45
  22.6 81.7 %reduce-scatter.2.cloned.1.call-start = ((), (), s32[]{:S(2)}) async-start(), calls=%async_computation.3 | async-start | bytes 307200 | tf_op jit(solution)/shard_map/reduce_scatter | solution.py:63
  34.9 35.0 %copy-start.4 = (f32[2,2048]{1,0:T(2,128)S(1)}, f32[2,2048]{1,0:T(2,128)}, u32[]{:S(2)}) copy-start(f32[2,2048]{1,0:T(2,128)} %param.12) | copy-start | bytes 49156
  34.9 35.0 %copy-start.5 = (f32[2,2048]{1,0:T(2,128)S(1)}, f32[2,2048]{1,0:T(2,128)}, u32[]{:S(2)}) copy-start(f32[2,2048]{1,0:T(2,128)} %param.11) | copy-start | bytes 49156
  34.9 35.0 %copy-start.6 = (s32[2,2048]{1,0:T(2,128)S(1)}, s32[2,2048]{1,0:T(2,128)}, u32[]{:S(2)}) copy-start(s32[2,2048]{1,0:T(2,128)} %param.13) | copy-start | bytes 49156
  106.6 44.8 %copy-start.2 = (f32[51200]{0:T(1024)S(1)}, f32[51200]{0:T(1024)}, u32[]{:S(2)}) copy-start(f32[51200]{0:T(1024)} %param.8) | copy-start | bytes 614404
  106.6 39.9 %all-to-all-start.1 = ((bf16[16,2,1600]{2,1,0:T(2,128)(2,1)}), bf16[16,2,1600]{2,1,0:T(2,128)(2,1)S(1)}, u32[]{:S(2)}, u32[]{:S(2)}) async-start(bf16[16,2,1600]{2,1,0:T(2,128)(2,1)} %reshape.141), calls=%async_computation.2 | async-start | bytes 212992 | tf_op jit(solution)/shard_map/all_to_all | solution.py:71
  146.7 4.7 %copy-start.1 = (f32[1,51200]{1,0:T(1,128)S(1)}, f32[1,51200]{1,0:T(1,128)}, u32[]{:S(2)}) copy-start(f32[1,51200]{1,0:T(1,128)} %param.7) | copy-start | bytes 614404
Sparse Core Ops, SparseCore 0:
  95.0 9.2 reduce-scatter.1
